TPU v7x, 32 devices: a whole 2x2x4 slice. The times are simulated.
32 devices in a mesh: blk: 8 (over y, x, core), ab: 4 (over z).
Axes of the slice: x: 2, y: 2, z: 4, core: 2. Of those that a mesh axis runs over, the one named last changes fastest.
Arguments:
- amplitudes: bfloat16 [512, 11264], P('blk'), may hold values from -6 to 6
- integrals: bfloat16 [4096, 11264], P(('blk', 'ab')), may hold values from -0.0546875 to 0.0546875
- live_rows: int32 [8], replicated, may hold values from 1 to 64, 320 in all
- partner: int32 [512], replicated, may hold values from 0 to 511, as said below
Outputs:
- ladder: float32 [512, 4096], P(None, ('blk', 'ab'))
Inputs may be any that keep to these rules, and one draw needn't show every extreme that they name: `live_rows`: lengths of the blocks; the largest equals 64. An involution without fixed points: partner[partner[r]] = r and partner[r] != r.
All inputs are finite; a program needn't handle non-finite values.
Results may differ from a plain program's by a relative error of at most 0.0003.
Values may be sent and summed in bfloat16 or wider, within the bound.
A program may use at most 128 MiB of HBM per device.

v0:
```python
import jax
import jax.numpy as jnp
from jax import lax
from jax.sharding import PartitionSpec as P


def passed_along(block, axis, distance):
    devices = range(lax.axis_size(axis))
    route = [((i - distance) % len(devices), i) for i in devices]
    return lax.ppermute(block, axis, route)


def block_product(rows, integrals):
    return lax.dot_general(
        rows, integrals, (((1,), (1,)), ((), ())), preferred_element_type=jnp.float32
    )


def shards(amplitudes, integrals, live_rows, partner):
    height = amplitudes.shape[0]
    count = lax.axis_size("blk")
    total = height * count
    partial_w = block_product(lax.all_gather(amplitudes, "blk", axis=0, tiled=True), integrals)
    slots = jnp.arange(total, dtype=jnp.int32)
    live = slots % height < jnp.repeat(live_rows, height, total_repeat_length=total)
    partial_w = jnp.where(live[:, None], partial_w, jnp.zeros_like(partial_w))
    mated = passed_along(partial_w, "ab", lax.axis_size("ab") // 2)
    return partial_w + mated[partner]


def solution(mesh):
    return jax.shard_map(
        shards,
        mesh=mesh,
        in_specs=(P("blk", None), P(("blk", "ab"), None), P(), P()),
        out_specs=P(None, ("blk", "ab")),
        check_vma=False,
    )
```

profile of v0, /device:TPU:0, one launch (start us, length us, event | category | flops | bytes accessed | tf_op | source)
XLA Modules:
  0.0 110.2 jit_solution(1682884423130123237)
XLA Ops:
  6.5 0.0 copy-start
  6.5 0.0 all-gather.2.cloned.1.call-start
  6.5 0.7 all-gather.2.cloned.1.call-update
  7.3 1.6 %fusion.4 = (s32[1]{0:T(128)}, s32[1]{0:T(128)}, s32[1]{0:T(128)}, s32[1]{0:T(128)}, s32[1]{0:T(128)}, /*index=5*/s32[1]{0:T(128)}, s32[1]{0:T(128)}, s32[1]{0:T(128)}) fusion(s32[8]{0:T(128)} %param.8), kind=kLoop, calls=%fused_computation.23 | loop fusion | bytes 64 | tf_op jit(solution)/shard_map/jit(_take)/gather | solution.py:25
  8.9 0.8 add_add_fusion.1
  9.7 4.4 %compare_select_fusion.1 = s32[512,1]{0,1:T(1,128)S(1)} fusion(s32[]{:T(128)} %bitcast.5, s32[]{:T(128)} %bitcast.6, s32[]{:T(128)} %bitcast.7, s32[]{:T(128)} %bitcast.8, s32[]{:T(128)} %bitcast.9, s32[]{:T(128)} %bitcast.11, s32[]{:T(128)} %bitcast.10, s32[512,1]{0,1:T(1,128)S(1)} %bitcast.24, s32[512,1]{0,1:T(1,128)S(1)} %bitcast.22), kind=kLoop, calls=%fused_computation.4 | loop fusion | flops 7168 | bytes 6172 | tf_op jit(solution)/shard_map/jit(_take)/gather | solution.py:25
  14.1 1.4 %fusion = pred[512]{0:T(512)(128)(4,1)S(1)} fusion(pred[512]{0:T(512)(128)(4,1)S(1)} %compare_reduce_fusion, s32[512]{0:T(512)S(1)} %bitcast.25, s32[]{:T(128)} %bitcast.4, s32[4,128]{1,0:T(4,128)} %constant.101.clone.1, s32[4]{0:T(128)S(1)} %iota_multiply_fusion), kind=kLoop, calls=%fused_computation.16 | loop fusion | flops 8704 | bytes 5140 | tf_op jit(solution)/shard_map/lt | solution.py:25
  15.5 0.0 copy-start.2
  15.5 64.0 %all-gather.2.cloned.1.call-done = bf16[512,11264]{1,0:T(8,128)(2,1)} async-done(((bf16[64,11264]{1,0:T(8,128)(2,1)}), bf16[512,11264]{1,0:T(8,128)(2,1)}) %all-gather.2.cloned.1.call-update) | async-done | bytes 11534352 | tf_op jit(solution)/shard_map/all_gather | solution.py:23
  79.5 0.0 copy-done
  79.5 6.0 %convolution_select_fusion = f32[512,128]{1,0:T(8,128)S(1)} fusion(bf16[512,11264]{1,0:T(8,128)(2,1)} %all-gather.2.cloned.1.call-done, bf16[128,11264]{1,0:T(8,128)(2,1)S(1)} %copy-done, pred[512]{0:T(512)(128)(4,1)S(1)} %fusion), kind=kOutput, calls=%fused_computation.1 | convolution fusion | flops 1476460544 | bytes 14680576 | tf_op jit(solution)/shard_map/dot_general | solution.py:14
  85.6 0.0 copy-start.1
  85.6 2.5 %collective-permute-start = (f32[512,128]{1,0:T(8,128)S(1)}, f32[512,128]{1,0:T(8,128)S(1)}, u32[]{:S(2)}, u32[]{:S(2)}) collective-permute-start(f32[512,128]{1,0:T(8,128)S(1)} %convolution_select_fusion), channel_id=1, source_target_pairs={{2,0},{3,1},{0,2},{1,3},{6,4},{7,5},{4,6},{5,7},{10,8},{11,9},{8,1... | collective-permute-start | bytes 786440 | tf_op jit(solution)/shard_map/ppermute | solution.py:10
  88.0 0.0 copy-done.2
  88.1 0.0 copy-done.1
  88.1 12.5 %collective-permute-done = f32[512,128]{1,0:T(8,128)S(1)} collective-permute-done((f32[512,128]{1,0:T(8,128)S(1)}, f32[512,128]{1,0:T(8,128)S(1)}, u32[]{:S(2)}, u32[]{:S(2)}) %collective-permute-start) | collective-permute-done | bytes 262176 | tf_op jit(solution)/shard_map/ppermute | solution.py:10
  100.6 1.0 gather_fusion
  101.6 1.7 %add.80 = f32[512,128]{1,0:T(8,128)} add(f32[512,128]{1,0:T(8,128)} %copy-done.1, f32[512,128]{1,0:T(8,128)S(1)} %gather_fusion) | non-fusion elementwise | flops 65536 | bytes 786432 | tf_op jit(solution)/shard_map/add | solution.py:28
  (4 shorter events, 0.0 us)
Async XLA Ops:
  6.5 73.0 %copy-start = (bf16[128,11264]{1,0:T(8,128)(2,1)S(1)}, bf16[128,11264]{1,0:T(8,128)(2,1)}, u32[]{:S(2)}) copy-start(bf16[128,11264]{1,0:T(8,128)(2,1)} %param.7) | copy-start | bytes 8650756
  6.5 73.0 %all-gather.2.cloned.1.call-start = ((), (), s32[]{:S(2)}) async-start(), calls=%async_computation | async-start | bytes 12976128 | tf_op jit(solution)/shard_map/all_gather | solution.py:23
  15.5 72.5 %copy-start.2 = (s32[512]{0:T(512)S(1)}, s32[512]{0:T(512)}, u32[]{:S(2)}) copy-start(s32[512]{0:T(512)} %param.9) | copy-start | bytes 6148
  85.6 2.5 %copy-start.1 = (f32[512,128]{1,0:T(8,128)}, f32[512,128]{1,0:T(8,128)S(1)}, u32[]{:S(2)}) copy-start(f32[512,128]{1,0:T(8,128)S(1)} %convolution_select_fusion) | copy-start | bytes 786436
  85.6 15.0 %collective-permute-start = (f32[512,128]{1,0:T(8,128)S(1)}, f32[512,128]{1,0:T(8,128)S(1)}, u32[]{:S(2)}, u32[]{:S(2)}) collective-permute-start(f32[512,128]{1,0:T(8,128)S(1)} %convolution_select_fusion), channel_id=1, source_target_pairs={{2,0},{3,1},{0,2},{1,3},{6,4},{7,5},{4,6},{5,7},{10,8},{11,9},{8,1... | collective-permute-start | bytes 786440 | tf_op jit(solution)/shard_map/ppermute | solution.py:10
Sparse Core Ops, SparseCore 0:
  9.2 70.2 all-gather.1
where the time goes:
time: 110 us
  waiting for transfers between devices  77.3 us (70%)
  between operations  13.4 us (12%)
  other arithmetic  8.35 us (8%)
  matrix products  6 us (5%)
  local copies, waits for them, and re-layouts  2.67 us (2%)
  starting transfers between devices  2.47 us (2%)
    all_gather x1, waiting for transfers between devices, shards(): lax.all_gather(amplitudes, 'blk', axis=0, tiled=True)  64 us
    ppermute x1, waiting for transfers between devices, passed_along(): return lax.ppermute(block, axis, route)  12.5 us
    dot_general x1, matrix products, block_product(): lax.dot_general(rows, integrals, (((1,), (1,)), ((), ())), preferred_elem...  6 us
    gather x2, other arithmetic, shards(): jnp.repeat(live_rows, height, total_repeat_length=total)  4.48 us
    ppermute x1, starting transfers between devices, passed_along(): return lax.ppermute(block, axis, route)  2.47 us
  transfers between devices with their start and end apart: 2, of which 2 were waited for; matrix products, arithmetic and copies ran while one was open for 8% of the time, Pallas kernels for 0%

commit v1 on v0

v1 whole, which is shorter than its diff:
```python
import functools

import jax
import jax.numpy as jnp
from jax import lax
from jax.experimental import pallas as pl
from jax.experimental.pallas import tpu as pltpu
from jax.sharding import PartitionSpec as P

CUBE = 8
QUARTERS = 4
PIECES = 4
LAG_RELAY = 1
LAG_DOT = 2

OWN, FIRST, SECOND, ACROSS = 0, 1, 2, 3
SOURCE = {1: 0, 4: 0, 2: 1, 3: 1, 5: 1, 6: 2, 7: 3}


def kernel(
    height, depth, live_ref, partner_ref, a_ref, b_ref, out_ref,
    held, integrals, tile, mated,
    send_sem, recv_sem, own_sem, b_sem, mate_send, mate_recv,
):
    blk, ab = lax.axis_index("blk"), lax.axis_index("ab")
    ab_size = lax.axis_size("ab")
    b = lax.rem(blk, CUBE)
    base = blk - b
    core, x, y = lax.rem(b, 2), lax.rem(lax.div(b, 2), 2), lax.rem(lax.div(b, 4), 2)
    parity = lax.rem(ab, 2)
    flip = 1 - 2 * core
    near_x, near_y = b + 2 - 4 * x, b + 4 - 8 * y
    first = near_x + parity * (near_y - near_x)
    other = near_x + near_y - first
    diagonal = near_x + near_y - b
    blocks = [b, first, diagonal, other]
    blocks = blocks + [i + flip for i in blocks]
    to_first = (base + first, ab)
    to_second = (base + other, ab)
    to_across = (blk, ab + 1 - 2 * parity)
    to_sibling = (blk + flip, ab)
    to_mate = (blk, lax.rem(ab + ab_size // 2, ab_size))
    target = {1: to_first, 2: to_second, 3: to_across}
    target.update({slot: to_sibling for slot in (4, 5, 6, 7)})

    rows = a_ref.shape[0] // QUARTERS
    steps = QUARTERS * PIECES

    def where(t):
        return t // PIECES, pl.ds((t % PIECES) * depth, depth)

    def remote(slot, t):
        q, columns = where(t)
        if SOURCE[slot] == OWN:
            src = a_ref.at[pl.ds(q * rows, rows), columns]
        else:
            src = held.at[q, SOURCE[slot], :, columns]
        return pltpu.make_async_remote_copy(
            src_ref=src,
            dst_ref=held.at[q, slot, :, columns],
            send_sem=send_sem.at[slot, t],
            recv_sem=recv_sem.at[slot, t],
            device_id=target[slot],
            device_id_type=pl.DeviceIdType.MESH,
        )

    def mate(q):
        band = pl.ds(q * rows, rows)
        return pltpu.make_async_remote_copy(
            src_ref=tile.at[:, band, :],
            dst_ref=mated.at[:, band, :],
            send_sem=mate_send.at[q],
            recv_sem=mate_recv.at[q],
            device_id=to_mate,
            device_id_type=pl.DeviceIdType.MESH,
        )

    def load_b(k):
        columns = pl.ds(k * depth, depth)
        return pltpu.make_async_copy(b_ref.at[:, columns], integrals.at[:, columns], b_sem.at[k])

    def load_own(q):
        return pltpu.make_async_copy(a_ref.at[pl.ds(q * rows, rows), :], held.at[q, OWN], own_sem.at[q])

    barrier = pltpu.get_barrier_semaphore()
    neighbours = (to_first, to_second, to_across, to_sibling, to_mate)
    for device in neighbours:
        pl.semaphore_signal(barrier, inc=1, device_id=device, device_id_type=pl.DeviceIdType.MESH)
    pl.semaphore_wait(barrier, len(neighbours))

    for t in range(steps):
        remote(1, t).start()
        remote(4, t).start()
    for k in range(PIECES):
        load_b(k).start()
    for q in range(QUARTERS):
        load_own(q).start()

    total = None
    for step in range(steps + LAG_DOT):
        if step < steps:
            remote(1, step).wait_recv()
            for slot in (2, 3, 5):
                remote(slot, step).start()
        t = step - LAG_RELAY
        if 0 <= t < steps:
            remote(2, t).wait_recv()
            remote(6, t).start()
            remote(3, t).wait_recv()
            remote(7, t).start()
        t = step - LAG_DOT
        if t >= 0:
            q, columns = where(t)
            k = t % PIECES
            if k == 0:
                load_own(q).wait()
            if q == 0:
                load_b(k).wait()
            for slot in (4, 5, 6, 7):
                remote(slot, t).wait_recv()
            left = held[q, :, :, columns].reshape(CUBE * rows, depth)
            product = lax.dot_general(
                left, integrals[:, columns], (((1,), (1,)), ((), ())),
                preferred_element_type=jnp.float32,
            )
            total = product if k == 0 else total + product
            if k == PIECES - 1:
                group, inside = (q * rows) // height, (q * rows) % height
                repeats = a_ref.shape[0] // height
                row = inside + lax.broadcasted_iota(jnp.int32, (rows, total.shape[1]), 0)
                for slot in range(CUBE):
                    part = total[slot * rows:(slot + 1) * rows]
                    limit = live_ref[blocks[slot] * repeats + group]
                    tile[blocks[slot], pl.ds(q * rows, rows), :] = jnp.where(row < limit, part, 0.0)
                mate(q).start()

    for q in range(QUARTERS):
        mate(q).wait_recv()
    span = a_ref.shape[0]
    for i in range(CUBE):
        @pl.loop(0, span, step=8)
        def _(r):
            r = pl.multiple_of(r, 8)
            picked = []
            for j in range(8):
                p = partner_ref[i * span + r + j]
                picked.append(mated[lax.div(p, span), pl.ds(lax.rem(p, span), 1), :])
            out_ref[i, pl.ds(r, 8), :] = tile[i, pl.ds(r, 8), :] + jnp.concatenate(picked, axis=0)
    for q in range(QUARTERS):
        mate(q).wait_send()
    for t in range(steps):
        for slot in SOURCE:
            remote(slot, t).wait_send()


def shards(amplitudes, integrals, live_rows, partner):
    height, length = amplitudes.shape
    wide = integrals.shape[0]
    count = lax.axis_size("blk")
    repeats = count // CUBE
    if repeats > 1:
        groups = [[i + CUBE * j for j in range(repeats)] for i in range(CUBE)]
        amplitudes = lax.all_gather(amplitudes, "blk", axis=0, axis_index_groups=groups, tiled=True)
        live_rows = live_rows.reshape(repeats, CUBE).T.reshape(-1)
        block = partner // height
        partner = ((block % CUBE) * repeats + block // CUBE) * height + partner % height
        partner = partner.reshape(repeats, CUBE, height).transpose(1, 0, 2).reshape(-1)
    span = height * repeats
    rows = span // QUARTERS
    steps = QUARTERS * PIECES
    out = pl.pallas_call(
        functools.partial(kernel, height, length // PIECES),
        out_shape=jax.ShapeDtypeStruct((CUBE, span, wide), jnp.float32),
        in_specs=[
            pl.BlockSpec(memory_space=pltpu.SMEM),
            pl.BlockSpec(memory_space=pltpu.SMEM),
            pl.BlockSpec(memory_space=pl.ANY),
            pl.BlockSpec(memory_space=pl.ANY),
        ],
        out_specs=pl.BlockSpec(memory_space=pltpu.VMEM),
        scratch_shapes=[
            pltpu.VMEM((QUARTERS, CUBE, rows, length), jnp.bfloat16),
            pltpu.VMEM((wide, length), jnp.bfloat16),
            pltpu.VMEM((CUBE, span, wide), jnp.float32),
            pltpu.VMEM((CUBE, span, wide), jnp.float32),
            pltpu.SemaphoreType.DMA((CUBE, steps)),
            pltpu.SemaphoreType.DMA((CUBE, steps)),
            pltpu.SemaphoreType.DMA((QUARTERS,)),
            pltpu.SemaphoreType.DMA((PIECES,)),
            pltpu.SemaphoreType.DMA((QUARTERS,)),
            pltpu.SemaphoreType.DMA((QUARTERS,)),
        ],
        compiler_params=pltpu.CompilerParams(
            collective_id=0, has_side_effects=True, vmem_limit_bytes=56 * 1024 * 1024
        ),
    )(live_rows, partner, amplitudes, integrals)
    if repeats > 1:
        out = out.reshape(CUBE, repeats, height, wide).transpose(1, 0, 2, 3)
    return out.reshape(count * height, wide)


def solution(mesh):
    return jax.shard_map(
        shards,
        mesh=mesh,
        in_specs=(P("blk", None), P(("blk", "ab"), None), P(), P()),
        out_specs=P(None, ("blk", "ab")),
        check_vma=False,
    )
```

time: 110 us -> 64.5 us (0.59)
  waiting for transfers between devices: 77.3 us -> 0 us
  Pallas kernels: 0 us -> 62.7 us
  between operations: 13.4 us -> 0.01 us
  other arithmetic: 8.35 us -> 0 us
  matrix products: 6 us -> 0 us
  starting transfers between devices: 2.47 us -> 0 us
    all_gather x1 -> x0, waiting for transfers between devices: 64 us -> none  [shards(): lax.all_gather(amplitudes, 'blk', axis=0, tiled=True)]
    pallas_call x0 -> x1, Pallas kernels: none -> 62.7 us  [shards(): pl.pallas_call(functools.partial(kernel, height, length // PIECES), out_s...]
    ppermute x1 -> x0, waiting for transfers between devices: 12.5 us -> none  [passed_along(): return lax.ppermute(block, axis, route)]
    dot_general x1 -> x0, matrix products: 6 us -> none  [block_product(): lax.dot_general(rows, integrals, (((1,), (1,)), ((), ())), preferred_elem...]
    gather x3 -> x0, other arithmetic: 4.48 us -> none  [the longest x2 4.48 us: shards(): jnp.repeat(live_rows, height, total_repeat_length=total)]
    gather x2 -> x0, local copies, waits for them, and re-layouts: 2.66 us -> none  [the longest x1 1.63 us: shards(): jnp.repeat(live_rows, height, total_repeat_length=total)]
    ppermute x1 -> x0, starting transfers between devices: 2.47 us -> none  [passed_along(): return lax.ppermute(block, axis, route)]
    add x1 -> x0, other arithmetic: 1.7 us -> none  [shards(): return partial_w + mated[partner]]
  transfers between devices with their start and end apart: 2 -> 0, of which waited for: 2 -> 0; matrix products, arithmetic and copies ran while one was open for 8% -> 0% of each run, Pallas kernels for 0% -> 0%
where the time goes in v1:
time: 64.5 us; the launch traced here: 64.3 us
  Pallas kernels  62.7 us (97%)
  local copies, waits for them, and re-layouts  1.67 us (3%)
    pallas_call x1, Pallas kernels, shards(): pl.pallas_call(functools.partial(kernel, height, length // PIECES), out_s...  62.7 us
    unnamed x1, local copies, waits for them, and re-layouts  1.67 us

profile of v1, /device:TPU:0, one launch (start us, length us, event | category | flops | bytes accessed | tf_op | source)
XLA Modules:
  0.0 64.3 jit_solution(4487157300319296905)
XLA Ops:
  0.0 62.7 %shard_map.46 = f32[8,64,128]{2,1,0:T(8,128)} custom-call(s32[8]{0:T(128)} %live_ref.1, s32[512]{0:T(512)} %partner_ref.1, bf16[64,11264]{1,0:T(8,128)(2,1)} %a_ref.1, bf16[128,11264]{1,0:T(8,128)(2,1)} %b_ref.1), custom_call_target="tpu_custom_call" | custom-call | tf_op jit(solution)/shard_map/pallas_call | solution.py:171
  62.7 1.7 %copy.6 = f32[512,128]{1,0:T(8,128)} copy(f32[512,128]{1,0:T(8,128)} %bitcast.1) | data formatting | bytes 524288

commit v2 on v1

v2 whole, which is shorter than its diff:
```python
import functools

import jax
import jax.numpy as jnp
from jax import lax
from jax.experimental import pallas as pl
from jax.experimental.pallas import tpu as pltpu
from jax.sharding import PartitionSpec as P

CUBE = 8
QUARTERS = 4
PIECES = 4
DIRECT = 2
SWAPPED = 1
WINDOW = 8
TURN = 6
LAG_RELAY = 3
LAG_DOT = 4

OWN, TWIN, FIRST, SECOND, ACROSS, TWIN_FIRST, TWIN_SECOND, TWIN_ACROSS = range(CUBE)


def kernel(
    height, depth, live_ref, partner_ref, a_ref, b_ref, out_ref,
    held, integrals, tile, mated,
    send_sem, recv_sem, own_sem, b_sem, mate_send, mate_recv,
):
    blk, ab = lax.axis_index("blk"), lax.axis_index("ab")
    ab_size = lax.axis_size("ab")
    b = lax.rem(blk, CUBE)
    base = blk - b
    core, x, y = lax.rem(b, 2), lax.rem(lax.div(b, 2), 2), lax.rem(lax.div(b, 4), 2)
    parity = lax.rem(ab, 2)
    flip = 1 - 2 * core
    near_x, near_y = b + 2 - 4 * x, b + 4 - 8 * y
    first = near_x + parity * (near_y - near_x)
    other = near_x + near_y - first
    diagonal = near_x + near_y - b
    blocks = [b, b + flip, first, diagonal, other, first + flip, diagonal + flip, other + flip]
    pairs = [i - core for i in (b, first, diagonal, other)]
    to_first = (base + first, ab)
    to_second = (base + other, ab)
    to_across = (blk, ab + 1 - 2 * parity)
    to_twin = (blk + flip, ab)
    to_mate = (blk, lax.rem(ab + ab_size // 2, ab_size))

    span = a_ref.shape[0]
    rows = span // QUARTERS
    repeats = span // height
    steps = QUARTERS * PIECES
    direct = range(steps - DIRECT, steps)
    swapped = range(steps - SWAPPED, steps)

    def route(slot, t):
        if slot == TWIN:
            return OWN, to_twin
        if slot == FIRST:
            return OWN, to_first
        if slot == SECOND:
            return (ACROSS, to_first) if t in swapped else (FIRST, to_second)
        if slot == ACROSS:
            return (OWN, to_second) if t in direct else (FIRST, to_across)
        return slot - 3, to_twin

    def remote(slot, t):
        q, columns = t // PIECES, pl.ds((t % PIECES) * depth, depth)
        origin, device = route(slot, t)
        if origin == OWN:
            src = a_ref.at[pl.ds(q * rows, rows), columns]
        else:
            src = held.at[q, origin, :, columns]
        return pltpu.make_async_remote_copy(
            src_ref=src,
            dst_ref=held.at[q, slot, :, columns],
            send_sem=send_sem.at[slot, t],
            recv_sem=recv_sem.at[slot, t],
            device_id=device,
            device_id_type=pl.DeviceIdType.MESH,
        )

    def mate(pair, q):
        if pair == 0:
            index, band = 0, pl.ds(0, span)
        else:
            index, band = 1 + q * 3 + pair - 1, pl.ds(q * rows, rows)
        where = (pl.ds(pairs[pair], 2), band, slice(None))
        return pltpu.make_async_remote_copy(
            src_ref=tile.at[where],
            dst_ref=mated.at[where],
            send_sem=mate_send.at[index],
            recv_sem=mate_recv.at[index],
            device_id=to_mate,
            device_id_type=pl.DeviceIdType.MESH,
        )

    mates = [(0, 0)] + [(pair, q) for q in range(QUARTERS) for pair in (1, 2, 3)]

    def load_b(k):
        columns = pl.ds(k * depth, depth)
        return pltpu.make_async_copy(b_ref.at[:, columns], integrals.at[:, columns], b_sem.at[k])

    def load_own(q):
        return pltpu.make_async_copy(a_ref.at[pl.ds(q * rows, rows), :], held.at[q, OWN], own_sem.at[q])

    def times(left, k):
        return lax.dot_general(
            left, integrals[:, pl.ds(k * depth, depth)], (((1,), (1,)), ((), ())),
            preferred_element_type=jnp.float32,
        )

    def keep(slot, q, part):
        group, inside = (q * rows) // height, (q * rows) % height
        row = inside + lax.broadcasted_iota(jnp.int32, part.shape, 0)
        limit = live_ref[blocks[slot] * repeats + group]
        tile[blocks[slot], pl.ds(q * rows, rows), :] = jnp.where(row < limit, part, 0.0)

    for q in range(QUARTERS):
        load_own(q).start()
    for k in range(PIECES):
        load_b(k).start()

    barrier = pltpu.get_barrier_semaphore()
    neighbours = (to_first, to_second, to_across, to_twin, to_mate)
    for device in neighbours:
        pl.semaphore_signal(barrier, inc=1, device_id=device, device_id_type=pl.DeviceIdType.MESH)
    pl.semaphore_wait(barrier, len(neighbours))

    for t in range(WINDOW):
        remote(FIRST, t).start()
    for t in direct:
        remote(ACROSS, t).start()
    for k in range(PIECES):
        for q in range(QUARTERS):
            remote(TWIN, q * PIECES + k).start()

    early, total = None, None
    for step in range(steps + LAG_DOT):
        if step < steps:
            remote(FIRST, step).wait_recv()
            if step not in swapped:
                remote(SECOND, step).start()
            if step not in direct:
                remote(ACROSS, step).start()
            remote(TWIN_FIRST, step).start()
            if step + WINDOW < steps:
                remote(FIRST, step + WINDOW).start()
        if step == TURN:
            for t in direct:
                remote(ACROSS, t).wait_recv()
                if t in swapped:
                    remote(SECOND, t).start()
                remote(TWIN_ACROSS, t).start()
        t = step - LAG_RELAY
        if 0 <= t < steps:
            remote(SECOND, t).wait_recv()
            remote(TWIN_SECOND, t).start()
            if t not in direct:
                remote(ACROSS, t).wait_recv()
                remote(TWIN_ACROSS, t).start()
        k = step - 1
        if 0 <= k < PIECES:
            load_b(k).wait()
            for q in range(QUARTERS):
                if k == 0:
                    load_own(q).wait()
                remote(TWIN, q * PIECES + k).wait_recv()
            left = held[:, OWN:FIRST, :, pl.ds(k * depth, depth)].reshape(2 * span, depth)
            early = times(left, k) if k == 0 else early + times(left, k)
            if k == PIECES - 1:
                for q in range(QUARTERS):
                    for slot in (OWN, TWIN):
                        start = (2 * q + slot) * rows
                        keep(slot, q, early[start:start + rows])
                mate(0, 0).start()
        t = step - LAG_DOT
        if t >= 0:
            q, k = t // PIECES, t % PIECES
            for slot in (TWIN_FIRST, TWIN_SECOND, TWIN_ACROSS):
                remote(slot, t).wait_recv()
            left = held[q, FIRST:, :, pl.ds(k * depth, depth)].reshape((CUBE - 2) * rows, depth)
            total = times(left, k) if k == 0 else total + times(left, k)
            if k == PIECES - 1:
                for slot in range(FIRST, CUBE):
                    start = (slot - FIRST) * rows
                    keep(slot, q, total[start:start + rows])
                for pair in (1, 2, 3):
                    mate(pair, q).start()

    for pair, q in mates:
        mate(pair, q).wait_recv()
    for i in range(CUBE):
        @pl.loop(0, span, step=8)
        def _(r):
            r = pl.multiple_of(r, 8)
            picked = []
            for j in range(8):
                p = partner_ref[i * span + r + j]
                picked.append(mated[lax.div(p, span), pl.ds(lax.rem(p, span), 1), :])
            out_ref[i, pl.ds(r, 8), :] = tile[i, pl.ds(r, 8), :] + jnp.concatenate(picked, axis=0)
    for pair, q in mates:
        mate(pair, q).wait_send()
    for t in range(steps):
        for slot in range(TWIN, CUBE):
            remote(slot, t).wait_send()


def shards(amplitudes, integrals, live_rows, partner):
    height, length = amplitudes.shape
    wide = integrals.shape[0]
    count = lax.axis_size("blk")
    repeats = count // CUBE
    if repeats > 1:
        groups = [[i + CUBE * j for j in range(repeats)] for i in range(CUBE)]
        amplitudes = lax.all_gather(amplitudes, "blk", axis=0, axis_index_groups=groups, tiled=True)
        live_rows = live_rows.reshape(repeats, CUBE).T.reshape(-1)
        block = partner // height
        partner = ((block % CUBE) * repeats + block // CUBE) * height + partner % height
        partner = partner.reshape(repeats, CUBE, height).transpose(1, 0, 2).reshape(-1)
    span = height * repeats
    rows = span // QUARTERS
    steps = QUARTERS * PIECES
    out = pl.pallas_call(
        functools.partial(kernel, height, length // PIECES),
        out_shape=jax.ShapeDtypeStruct((CUBE, span, wide), jnp.float32),
        in_specs=[
            pl.BlockSpec(memory_space=pltpu.SMEM),
            pl.BlockSpec(memory_space=pltpu.SMEM),
            pl.BlockSpec(memory_space=pl.ANY),
            pl.BlockSpec(memory_space=pl.ANY),
        ],
        out_specs=pl.BlockSpec(memory_space=pltpu.VMEM),
        scratch_shapes=[
            pltpu.VMEM((QUARTERS, CUBE, rows, length), jnp.bfloat16),
            pltpu.VMEM((wide, length), jnp.bfloat16),
            pltpu.VMEM((CUBE, span, wide), jnp.float32),
            pltpu.VMEM((CUBE, span, wide), jnp.float32),
            pltpu.SemaphoreType.DMA((CUBE, steps)),
            pltpu.SemaphoreType.DMA((CUBE, steps)),
            pltpu.SemaphoreType.DMA((QUARTERS,)),
            pltpu.SemaphoreType.DMA((PIECES,)),
            pltpu.SemaphoreType.DMA((1 + 3 * QUARTERS,)),
            pltpu.SemaphoreType.DMA((1 + 3 * QUARTERS,)),
        ],
        compiler_params=pltpu.CompilerParams(
            collective_id=0, has_side_effects=True, vmem_limit_bytes=56 * 1024 * 1024
        ),
    )(live_rows, partner, amplitudes, integrals)
    if repeats > 1:
        out = out.reshape(CUBE, repeats, height, wide).transpose(1, 0, 2, 3)
    return out.reshape(count * height, wide)


def solution(mesh):
    return jax.shard_map(
        shards,
        mesh=mesh,
        in_specs=(P("blk", None), P(("blk", "ab"), None), P(), P()),
        out_specs=P(None, ("blk", "ab")),
        check_vma=False,
    )
```

time: 64.5 us -> 55.3 us (0.86)
  Pallas kernels: 62.7 us -> 53.4 us
    pallas_call x1, Pallas kernels: 62.7 us -> 53.4 us  [shards(): pl.pallas_call(functools.partial(kernel, height, length // PIECES), out_s...]
where the time goes in v2:
time: 55.3 us; the launch traced here: 55.1 us
  Pallas kernels  53.4 us (97%)
  local copies, waits for them, and re-layouts  1.67 us (3%)
    pallas_call x1, Pallas kernels, shards(): pl.pallas_call(functools.partial(kernel, height, length // PIECES), out_s...  53.4 us
    unnamed x1, local copies, waits for them, and re-layouts  1.67 us

profile of v2, /device:TPU:0, one launch (start us, length us, event | category | flops | bytes accessed | tf_op | source)
XLA Modules:
  0.0 55.1 jit_solution(9570865115438349833)
XLA Ops:
  0.0 53.4 %shard_map.46 = f32[8,64,128]{2,1,0:T(8,128)} custom-call(s32[8]{0:T(128)} %live_ref.1, s32[512]{0:T(512)} %partner_ref.1, bf16[64,11264]{1,0:T(8,128)(2,1)} %a_ref.1, bf16[128,11264]{1,0:T(8,128)(2,1)} %b_ref.1), custom_call_target="tpu_custom_call" | custom-call | tf_op jit(solution)/shard_map/pallas_call | solution.py:222
  53.5 1.7 %copy.6 = f32[512,128]{1,0:T(8,128)} copy(f32[512,128]{1,0:T(8,128)} %bitcast.1) | data formatting | bytes 524288

commit v3 on v2

--- a/solution.py
+++ b/solution.py
@@ -14,8 +14,8 @@
 SWAPPED = 1
 WINDOW = 8
 TURN = 6
-LAG_RELAY = 3
-LAG_DOT = 4
+LAG_RELAY = 4
+LAG_DOT = 6
 
 OWN, TWIN, FIRST, SECOND, ACROSS, TWIN_FIRST, TWIN_SECOND, TWIN_ACROSS = range(CUBE)
 

time: 55.3 us -> 54.8 us (level)
  no operation moved by 1% of the time
where the time goes in v3:
time: 54.8 us; the launch traced here: 54.6 us
  Pallas kernels  53 us (97%)
  local copies, waits for them, and re-layouts  1.67 us (3%)
    pallas_call x1, Pallas kernels, shards(): pl.pallas_call(functools.partial(kernel, height, length // PIECES), out_s...  53 us
    unnamed x1, local copies, waits for them, and re-layouts  1.67 us

profile of v3, /device:TPU:0, one launch (start us, length us, event | category | flops | bytes accessed | tf_op | source)
XLA Modules:
  0.0 54.6 jit_solution(4509997383581378139)
XLA Ops:
  0.0 53.0 %shard_map.46 = f32[8,64,128]{2,1,0:T(8,128)} custom-call(s32[8]{0:T(128)} %live_ref.1, s32[512]{0:T(512)} %partner_ref.1, bf16[64,11264]{1,0:T(8,128)(2,1)} %a_ref.1, bf16[128,11264]{1,0:T(8,128)(2,1)} %b_ref.1), custom_call_target="tpu_custom_call" | custom-call | tf_op jit(solution)/shard_map/pallas_call | solution.py:222
  53.0 1.7 %copy.6 = f32[512,128]{1,0:T(8,128)} copy(f32[512,128]{1,0:T(8,128)} %bitcast.1) | data formatting | bytes 524288
